TPU v7x, 32 devices: a whole 2x2x4 slice. The times are simulated.
32 devices in a mesh: dp: 4 (over y, x), filter: 8 (over z, core).
Axes of the slice: x: 2, y: 2, z: 4, core: 2. Of those that a mesh axis runs over, the one named last changes fastest.
Arguments:
- fields: bfloat16 [4, 32, 32, 1024], P('dp', None, None, 'filter'), may hold values from -6 to 6
- weight_one: bfloat16 [3, 3, 1024, 1024], P(None, None, 'dp', 'filter'), may hold values from -0.0625 to 0.0625
- weight_two: bfloat16 [3, 3, 1024, 1024], P(None, None, 'dp', 'filter'), may hold values from -0.0625 to 0.0625
- cotangent: bfloat16 [4, 32, 32, 1024], P('dp', None, None, 'filter'), may hold values from -6 to 6
Outputs:
- output: bfloat16 [4, 32, 32, 1024], P('dp', None, None, 'filter')
- grad_one: float32 [3, 3, 1024, 1024], P(None, None, 'dp', 'filter')
- grad_two: float32 [3, 3, 1024, 1024], P(None, None, 'dp', 'filter')
All inputs are finite; a program needn't handle non-finite values.
Results may differ from a plain program's by a relative error of at most 0.018.
Values may be sent and summed in bfloat16 or wider, within the bound.
No kernel may reach another device: no remote copies, remote signals or barrier semaphores. Data moves between devices by JAX's collectives and lax.ppermute only.
A program may use at most 128 MiB of HBM per device.

v0:
```python
import jax
import jax.numpy as jnp
from jax import lax
from jax.sharding import PartitionSpec as P


def shift_cells(values, row_step, col_step):
    size = values.shape[1]
    padded = jnp.pad(values, ((0, 0), (1, 1), (1, 1), (0, 0)))
    return padded[:, 1 + row_step : 1 + row_step + size, 1 + col_step : 1 + col_step + size, :]


def conv_taps(inputs, weights):
    products = jnp.einsum("bhwc,pqcd->bhwpqd", inputs, weights, preferred_element_type=jnp.float32)
    result = jnp.zeros(inputs.shape[:3] + (weights.shape[3],), jnp.float32)
    for row_tap in range(3):
        for col_tap in range(3):
            result = result + shift_cells(
                products[:, :, :, row_tap, col_tap, :], row_tap - 1, col_tap - 1
            )
    return result


def shifted_stack(grads):
    pieces = []
    for row_tap in range(3):
        for col_tap in range(3):
            pieces.append(shift_cells(grads, 1 - row_tap, 1 - col_tap))
    return jnp.stack(pieces, axis=3).reshape(grads.shape[:3] + (3, 3, grads.shape[3]))


def transposed(grads, weights):
    stacked = shifted_stack(grads)
    return jnp.einsum("bhwpqd,pqcd->bhwc", stacked, weights, preferred_element_type=jnp.float32)


def filter_grads(inputs, grads):
    stacked = shifted_stack(grads)
    return jnp.einsum("bhwc,bhwpqd->pqcd", inputs, stacked, preferred_element_type=jnp.float32)


def body(fields, weight_one, weight_two, cotangent):
    full_one = lax.all_gather(weight_one, "dp", axis=2, tiled=True)
    gathered = lax.all_gather(fields, "filter", axis=3, tiled=True)
    pre_one = conv_taps(gathered, full_one)
    hidden = jax.nn.silu(pre_one).astype(jnp.bfloat16)
    hidden_all = lax.all_gather(hidden, "filter", axis=3, tiled=True)
    full_two = lax.all_gather(weight_two, "dp", axis=2, tiled=True)
    output = conv_taps(hidden_all, full_two).astype(jnp.bfloat16)
    grad_two = lax.psum_scatter(
        filter_grads(hidden_all, cotangent).astype(jnp.bfloat16),
        "dp",
        scatter_dimension=2,
        tiled=True,
    ).astype(jnp.float32)
    partial_back = transposed(cotangent, full_two)
    back = lax.psum_scatter(
        partial_back.astype(jnp.bfloat16), "filter", scatter_dimension=3, tiled=True
    ).astype(jnp.float32)
    sigma = jax.nn.sigmoid(pre_one)
    back_pre = (back * sigma * (1.0 + pre_one * (1.0 - sigma))).astype(jnp.bfloat16)
    grad_one = lax.psum_scatter(
        filter_grads(gathered, back_pre).astype(jnp.bfloat16), "dp", scatter_dimension=2, tiled=True
    ).astype(jnp.float32)
    return (output, grad_one, grad_two)


def solution(mesh):
    placed = (
        P("dp", None, None, "filter"),
        P(None, None, "dp", "filter"),
        P(None, None, "dp", "filter"),
        P("dp", None, None, "filter"),
    )
    return jax.shard_map(
        body,
        mesh=mesh,
        in_specs=placed,
        out_specs=(
            P("dp", None, None, "filter"),
            P(None, None, "dp", "filter"),
            P(None, None, "dp", "filter"),
        ),
        check_vma=False,
    )
```

profile of v0, /device:TPU:0, one launch (start us, length us, event | category | flops | bytes accessed | tf_op | source)
XLA Modules:
  0.0 284.4 jit_solution(1730159838617975054)
XLA Ops:
  12.1 38.0 %all-gather.11.cloned.1.call-done = bf16[3,3,1024,128]{3,2,1,0:T(8,128)(2,1)} async-done(((bf16[3,3,256,128]{3,2,1,0:T(8,128)(2,1)}), bf16[3,3,1024,128]{3,2,1,0:T(8,128)(2,1)}) %all-gather.11.cloned.1.call-update) | async-done | bytes 2359312 | tf_op jit(solution)/shard_map/all_gather | solution.py:48
  50.1 5.3 %fusion.16 = bf16[1,32,32,1024]{3,2,1,0:T(8,128)(2,1)S(1)} fusion(bf16[32,32,3,3,128]{4,1,0,3,2:T(8,128)(2,1)} %bitcast.223, bf16[3,3,1024,128]{3,2,1,0:T(8,128)(2,1)} %all-gather.11.cloned.1.call-done), kind=kOutput, calls=%fused_computation.15 | convolution fusion | flops 2416967680 | bytes 6815744 | tf_op jit(solution)/shard_map/bhwpqd,pqcd->bhwc/dot_general | solution.py:34
  55.4 12.2 %copy.60 = bf16[1,32,32,1024]{2,1,0,3:T(8,128)(2,1)} copy(bf16[1,32,32,1024]{3,2,1,0:T(8,128)(2,1)S(1)} %fusion.16) | data formatting | bytes 4194304
  67.5 12.5 %reshape.42 = bf16[1024,1024]{1,0:T(8,128)(2,1)} reshape(bf16[1024,1,32,32]{3,2,1,0:T(8,128)(2,1)} %bitcast.220) | data formatting | bytes 4194304
  80.0 9.4 %all-gather.7.cloned.1.call-done = bf16[3,3,1024,128]{3,2,1,0:T(8,128)(2,1)} async-done(((bf16[3,3,256,128]{3,2,1,0:T(8,128)(2,1)}), bf16[3,3,1024,128]{3,2,1,0:T(8,128)(2,1)}) %all-gather.7.cloned.1.call-update) | async-done | bytes 2359312 | tf_op jit(solution)/shard_map/all_gather | solution.py:43
  89.4 32.5 %all-gather.5.cloned.1.call-done = bf16[1,32,32,1024]{3,2,1,0:T(8,128)(2,1)} async-done(((bf16[1,32,32,128]{3,2,1,0:T(8,128)(2,1)}), bf16[1,32,32,1024]{3,2,1,0:T(8,128)(2,1)}) %all-gather.5.cloned.1.call-update) | async-done | bytes 2097168 | tf_op jit(solution)/shard_map/all_gather | solution.py:44
  121.9 5.2 %fusion.10 = f32[1,32,32,3,3,128]{5,2,4,3,1,0:T(8,128)S(1)} fusion(bf16[3,3,1024,128]{3,2,1,0:T(8,128)(2,1)} %all-gather.7.cloned.1.call-done, bf16[1,32,32,1024]{3,2,1,0:T(8,128)(2,1)} %all-gather.5.cloned.1.call-done), kind=kOutput, calls=%fused_computation.13 | convolution fusion | flops 2415919104 | bytes 9175040 | tf_op jit(solution)/shard_map/bhwc,pqcd->bhwpqd/dot_general | solution.py:14
  127.1 2.1 copy-done.1
  129.2 1.8 slice_bitcast_fusion.17
  130.9 28.0 %reduce-scatter.10.cloned.1.call-done = bf16[128,1024]{1,0:T(8,128)(2,1)} async-done(((bf16[1024,1024]{1,0:T(8,128)(2,1)}), bf16[128,1024]{1,0:T(8,128)(2,1)}) %reduce-scatter.10.cloned.1.call-update) | async-done | bytes 262160
  158.9 1.8 reshape.43
  160.7 1.8 copy.61
  162.5 2.3 multiply_convert_fusion
  167.5 4.0 %fusion = bf16[3,3,1024,128]{2,3,1,0:T(8,128)(2,1)} fusion(bf16[32,32,3,3,128]{4,1,0,3,2:T(8,128)(2,1)S(1)} %bitcast.225, bf16[1,32,32,1024]{3,2,1,0:T(8,128)(2,1)S(1)} %copy-done.5), kind=kOutput, calls=%fused_computation.3 | convolution fusion | flops 2417098752 | bytes 6815744 | tf_op jit(solution)/shard_map/bhwc,bhwpqd->pqcd/dot_general | solution.py:39
  171.6 23.8 %all-gather.9.cloned.1.call-done = bf16[1,32,32,1024]{3,2,1,0:T(8,128)(2,1)} async-done(((bf16[1,32,32,128]{3,2,1,0:T(8,128)(2,1)}), bf16[1,32,32,1024]{3,2,1,0:T(8,128)(2,1)}) %all-gather.9.cloned.1.call-update) | async-done | bytes 2097168 | tf_op jit(solution)/shard_map/all_gather | solution.py:47
  195.4 4.2 %fusion.4 = bf16[3,3,128,1024,1]{3,2,0,1,4:T(8,128)(2,1)S(1)} fusion(bf16[32,32,3,3,128]{4,1,0,3,2:T(8,128)(2,1)S(1)} %bitcast.224, bf16[1,32,32,1024]{3,2,1,0:T(8,128)(2,1)} %all-gather.9.cloned.1.call-done), kind=kOutput, calls=%fused_computation.7 | convolution fusion | flops 2415919104 | bytes 6815744 | tf_op jit(solution)/shard_map/bhwc,bhwpqd->pqcd/dot_general | solution.py:39
  199.6 1.7 copy.83
  201.4 1.6 copy-done.4
  203.0 4.8 %fusion.13 = f32[1,32,32,3,3,128]{5,2,4,3,1,0:T(8,128)S(1)} fusion(bf16[3,3,1024,128]{3,2,1,0:T(8,128)(2,1)S(1)} %copy-done.4, bf16[1,32,32,1024]{3,2,1,0:T(8,128)(2,1)} %all-gather.9.cloned.1.call-done), kind=kOutput, calls=%fused_computation.14 | convolution fusion | flops 2415919104 | bytes 9175040 | tf_op jit(solution)/shard_map/bhwc,pqcd->bhwpqd/dot_general | solution.py:14
  208.5 1.3 fusion.39
  209.8 25.0 %reduce-scatter.6.cloned.1.call-done = bf16[3,3,256,128]{2,3,1,0:T(8,128)(2,1)} async-done(((bf16[3,3,1024,128]{2,3,1,0:T(8,128)(2,1)}), bf16[3,3,256,128]{2,3,1,0:T(8,128)(2,1)}) %reduce-scatter.6.cloned.1.call-update) | async-done | bytes 589840 | tf_op jit(solution)/shard_map/reduce_scatter | solution.py:62
  234.8 2.3 copy.45
  237.1 38.2 %reduce-scatter.8.cloned.1.call-done = bf16[3,3,256,128]{2,3,1,0:T(8,128)(2,1)} async-done(((bf16[3,3,1024,128]{2,3,1,0:T(8,128)(2,1)}), bf16[3,3,256,128]{2,3,1,0:T(8,128)(2,1)}) %reduce-scatter.8.cloned.1.call-update) | async-done | bytes 589840 | tf_op jit(solution)/shard_map/reduce_scatter | solution.py:50
  275.3 2.3 copy.46
  (44 shorter events, 8.3 us)
Async XLA Ops:
  7.2 4.3 %copy-start = (bf16[1,32,32,128]{3,2,1,0:T(8,128)(2,1)S(1)}, bf16[1,32,32,128]{3,2,1,0:T(8,128)(2,1)}, u32[]{:S(2)}) copy-start(bf16[1,32,32,128]{3,2,1,0:T(8,128)(2,1)} %param.7) | copy-start | bytes 786436
  7.2 42.9 %all-gather.11.cloned.1.call-start = ((), (), s32[]{:S(2)}) async-start(), calls=%async_computation.6 | async-start | bytes 2949120 | tf_op jit(solution)/shard_map/all_gather | solution.py:48
  7.9 81.5 %all-gather.7.cloned.1.call-start = ((), (), s32[]{:S(2)}) async-start(), calls=%async_computation.4 | async-start | bytes 2949120 | tf_op jit(solution)/shard_map/all_gather | solution.py:43
  8.7 113.2 %all-gather.5.cloned.1.call-start = ((), (), s32[]{:S(2)}) async-start(), calls=%async_computation.3 | async-start | bytes 2359296 | tf_op jit(solution)/shard_map/all_gather | solution.py:44
  9.4 149.5 %reduce-scatter.10.cloned.1.call-start = ((), (), s32[]{:S(2)}) async-start(), calls=%async_computation.9 | async-start | bytes 2359296
  12.1 38.0 %copy-start.2 = (bf16[1,32,32,9,128]{4,2,1,3,0:T(8,128)(2,1)}, bf16[1,32,32,9,128]{4,2,1,3,0:T(8,128)(2,1)S(1)}, u32[]{:S(2)}) copy-start(bf16[1,32,32,9,128]{4,2,1,3,0:T(8,128)(2,1)S(1)} %fusion.55) | copy-start | bytes 7077892
  80.0 115.4 %all-gather.9.cloned.1.call-start = ((), (), s32[]{:S(2)}) async-start(), calls=%async_computation.5 | async-start | bytes 2359296 | tf_op jit(solution)/shard_map/all_gather | solution.py:47
  127.1 2.1 copy-start.1
  165.7 69.1 %reduce-scatter.6.cloned.1.call-start = ((), (), s32[]{:S(2)}) async-start(), calls=%async_computation.7 | async-start | bytes 2949120 | tf_op jit(solution)/shard_map/reduce_scatter | solution.py:62
  165.9 1.6 copy-start.5
  171.5 23.9 %copy-start.3 = (bf16[1,32,32,9,128]{4,2,1,3,0:T(8,128)(2,1)S(1)}, bf16[1,32,32,9,128]{4,2,1,3,0:T(8,128)(2,1)}, u32[]{:S(2)}) copy-start(bf16[1,32,32,9,128]{4,2,1,3,0:T(8,128)(2,1)} %copy-done.2) | copy-start | bytes 7077892
  171.5 103.8 %reduce-scatter.8.cloned.1.call-start = ((), (), s32[]{:S(2)}) async-start(), calls=%async_computation.8 | async-start | bytes 2949120 | tf_op jit(solution)/shard_map/reduce_scatter | solution.py:50
  201.3 1.7 copy-start.4
Sparse Core Ops, SparseCore 0:
  9.9 40.1 all-gather.10
  51.9 37.4 all-gather.6
  91.0 30.8 all-gather.4
  124.0 34.8 reduce-scatter.9
  165.8 29.5 all-gather.8
  198.3 36.4 reduce-scatter.5
  237.9 37.3 reduce-scatter.7
where the time goes:
time: 285 us; the launch traced here: 284 us
  waiting for transfers between devices  197 us (69%)
  local copies, waits for them, and re-layouts  44.9 us (16%)
  matrix products  23.5 us (8%)
  between operations  14.3 us (5%)
  other arithmetic  4.4 us (2%)
    unnamed x34, local copies, waits for them, and re-layouts  40.6 us
    reduce_scatter x1, waiting for transfers between devices, body(): lax.psum_scatter(filter_grads(hidden_all, cotangent).astype(jnp.bfloat16)...  38.2 us
    all_gather x1, waiting for transfers between devices, body(): full_two = lax.all_gather(weight_two, 'dp', axis=2, tiled=True)  38 us
    all_gather x1, waiting for transfers between devices, body(): gathered = lax.all_gather(fields, 'filter', axis=3, tiled=True)  32.5 us
    unnamed x8, waiting for transfers between devices  30.1 us
    reduce_scatter x1, waiting for transfers between devices, body(): lax.psum_scatter(filter_grads(gathered, back_pre).astype(jnp.bfloat16), '...  25 us
    all_gather x1, waiting for transfers between devices, body(): hidden_all = lax.all_gather(hidden, 'filter', axis=3, tiled=True)  23.8 us
    dot_general x2, matrix products, conv_taps(): jnp.einsum('bhwc,pqcd->bhwpqd', inputs, weights, preferred_element_type=j...  9.99 us
  transfers between devices with their start and end apart: 7, of which 7 were waited for; matrix products, arithmetic and copies ran while one was open for 21% of the time, Pallas kernels for 0%

commit v1 on v0

--- a/solution.py
+++ b/solution.py
@@ -44,7 +44,16 @@
     gathered = lax.all_gather(fields, "filter", axis=3, tiled=True)
     pre_one = conv_taps(gathered, full_one)
     hidden = jax.nn.silu(pre_one).astype(jnp.bfloat16)
-    hidden_all = lax.all_gather(hidden, "filter", axis=3, tiled=True)
+    ways = lax.axis_size("filter")
+    up = [(d, (d + 1) % ways) for d in range(ways)]
+    down = [(d, (d - 1) % ways) for d in range(ways)]
+    earlier, later = ([hidden], [hidden])
+    for _ in range(ways // 2):
+        earlier.append(lax.ppermute(earlier[-1], "filter", up))
+    for _ in range((ways - 1) // 2):
+        later.append(lax.ppermute(later[-1], "filter", down))
+    line = jnp.concatenate([*earlier[::-1], *later[1:]], axis=3)
+    hidden_all = jnp.roll(line, (lax.axis_index("filter") - ways // 2) * hidden.shape[3], axis=3)
     full_two = lax.all_gather(weight_two, "dp", axis=2, tiled=True)
     output = conv_taps(hidden_all, full_two).astype(jnp.bfloat16)
     grad_two = lax.psum_scatter(

time: 285 us -> 256 us (0.90)
  waiting for transfers between devices: 197 us -> 158 us
  starting transfers between devices: 0.46 us -> 11.3 us
    reduce_scatter x1, waiting for transfers between devices: 25 us -> 0.01 us  [body(): lax.psum_scatter(filter_grads(gathered, back_pre).astype(jnp.bfloat16), '...]
    all_gather x1 -> x0, waiting for transfers between devices: 23.8 us -> none  [body(): hidden_all = lax.all_gather(hidden, 'filter', axis=3, tiled=True)]
    ppermute x0 -> x7, waiting for transfers between devices: none -> 20.1 us  [the longest x4 20.1 us: body(): earlier.append(lax.ppermute(earlier[-1], 'filter', up))]
    ppermute x0 -> x7, starting transfers between devices: none -> 10.9 us  [the longest x3 10.8 us: body(): later.append(lax.ppermute(later[-1], 'filter', down))]
    reduce_scatter x1, waiting for transfers between devices: 38.2 us -> 27.8 us  [body(): lax.psum_scatter(filter_grads(hidden_all, cotangent).astype(jnp.bfloat16)...]
    unnamed x34 -> x49, local copies, waits for them, and re-layouts: 40.6 us -> 41.8 us
    unnamed x8 -> x7, waiting for transfers between devices: 30.1 us -> 30.1 us
  transfers between devices with their start and end apart: 7 -> 13, of which waited for: 7 -> 9; matrix products, arithmetic and copies ran while one was open for 21% -> 21% of each run, Pallas kernels for 0% -> 0%
where the time goes in v1:
time: 256 us; the launch traced here: 255 us
  waiting for transfers between devices  158 us (62%)
  local copies, waits for them, and re-layouts  46.4 us (18%)
  matrix products  21.7 us (8%)
  between operations  14.4 us (6%)
  starting transfers between devices  11.3 us (4%)
  other arithmetic  4 us (2%)
    unnamed x49, local copies, waits for them, and re-layouts  41.8 us
    all_gather x1, waiting for transfers between devices, body(): full_two = lax.all_gather(weight_two, 'dp', axis=2, tiled=True)  38 us
    all_gather x1, waiting for transfers between devices, body(): gathered = lax.all_gather(fields, 'filter', axis=3, tiled=True)  32.5 us
    unnamed x7, waiting for transfers between devices  30.1 us
    reduce_scatter x1, waiting for transfers between devices, body(): lax.psum_scatter(filter_grads(hidden_all, cotangent).astype(jnp.bfloat16)...  27.8 us
    ppermute x4, waiting for transfers between devices, body(): earlier.append(lax.ppermute(earlier[-1], 'filter', up))  20.1 us
    ppermute x3, starting transfers between devices, body(): later.append(lax.ppermute(later[-1], 'filter', down))  10.8 us
    dot_general x2, matrix products, conv_taps(): jnp.einsum('bhwc,pqcd->bhwpqd', inputs, weights, preferred_element_type=j...  9.62 us
  transfers between devices with their start and end apart: 13, of which 9 were waited for; matrix products, arithmetic and copies ran while one was open for 21% of the time, Pallas kernels for 0%

profile of v1, /device:TPU:0, one launch (start us, length us, event | category | flops | bytes accessed | tf_op | source)
XLA Modules:
  0.0 255.4 jit_solution(13173618186684454433)
XLA Ops:
  12.1 38.0 %all-gather.8.cloned.1.call-done = bf16[3,3,1024,128]{3,2,1,0:T(8,128)(2,1)} async-done(((bf16[3,3,256,128]{3,2,1,0:T(8,128)(2,1)}), bf16[3,3,1024,128]{3,2,1,0:T(8,128)(2,1)}) %all-gather.8.cloned.1.call-update) | async-done | bytes 2359312 | tf_op jit(solution)/shard_map/all_gather | solution.py:57
  50.1 5.3 %fusion.16 = bf16[1,32,32,1024]{3,2,1,0:T(8,128)(2,1)S(1)} fusion(bf16[32,32,3,3,128]{4,1,0,3,2:T(8,128)(2,1)} %bitcast.223, bf16[3,3,1024,128]{3,2,1,0:T(8,128)(2,1)} %all-gather.8.cloned.1.call-done), kind=kOutput, calls=%fused_computation.15 | convolution fusion | flops 2416967680 | bytes 6815744 | tf_op jit(solution)/shard_map/bhwpqd,pqcd->bhwc/dot_general | solution.py:34
  55.4 12.2 %copy.60 = bf16[1,32,32,1024]{2,1,0,3:T(8,128)(2,1)} copy(bf16[1,32,32,1024]{3,2,1,0:T(8,128)(2,1)S(1)} %fusion.16) | data formatting | bytes 4194304
  67.5 12.4 %reshape.42 = bf16[1024,1024]{1,0:T(8,128)(2,1)} reshape(bf16[1024,1,32,32]{3,2,1,0:T(8,128)(2,1)} %bitcast.220) | data formatting | bytes 4194304
  80.2 9.2 %all-gather.6.cloned.1.call-done = bf16[3,3,1024,128]{3,2,1,0:T(8,128)(2,1)} async-done(((bf16[3,3,256,128]{3,2,1,0:T(8,128)(2,1)}), bf16[3,3,1024,128]{3,2,1,0:T(8,128)(2,1)}) %all-gather.6.cloned.1.call-update) | async-done | bytes 2359312 | tf_op jit(solution)/shard_map/all_gather | solution.py:43
  89.4 32.5 %all-gather.4.cloned.1.call-done = bf16[1,32,32,1024]{3,2,1,0:T(8,128)(2,1)} async-done(((bf16[1,32,32,128]{3,2,1,0:T(8,128)(2,1)}), bf16[1,32,32,1024]{3,2,1,0:T(8,128)(2,1)}) %all-gather.4.cloned.1.call-update) | async-done | bytes 2097168 | tf_op jit(solution)/shard_map/all_gather | solution.py:44
  121.9 5.2 %fusion.10 = f32[1,32,32,3,3,128]{5,2,4,3,1,0:T(8,128)S(1)} fusion(bf16[3,3,1024,128]{3,2,1,0:T(8,128)(2,1)} %all-gather.6.cloned.1.call-done, bf16[1,32,32,1024]{3,2,1,0:T(8,128)(2,1)} %all-gather.4.cloned.1.call-done), kind=kOutput, calls=%fused_computation.13 | convolution fusion | flops 2415919104 | bytes 9175040 | tf_op jit(solution)/shard_map/bhwc,pqcd->bhwpqd/dot_general | solution.py:14
  127.1 2.1 copy-done.1
  130.9 28.0 %reduce-scatter.10.cloned.1.call-done = bf16[128,1024]{1,0:T(8,128)(2,1)} async-done(((bf16[1024,1024]{1,0:T(8,128)(2,1)}), bf16[128,1024]{1,0:T(8,128)(2,1)}) %reduce-scatter.10.cloned.1.call-update) | async-done | bytes 262160
  158.9 1.8 reshape.43
  161.8 2.2 multiply_convert_fusion
  165.6 4.0 %fusion = bf16[3,3,1024,128]{2,3,1,0:T(8,128)(2,1)} fusion(bf16[32,32,3,3,128]{4,1,0,3,2:T(8,128)(2,1)S(1)} %bitcast.225, bf16[1,32,32,1024]{3,2,1,0:T(8,128)(2,1)S(1)} %copy-done.6), kind=kOutput, calls=%fused_computation.3 | convolution fusion | flops 2417098752 | bytes 6815744 | tf_op jit(solution)/shard_map/bhwc,bhwpqd->pqcd/dot_general | solution.py:39
  169.9 7.8 %collective-permute-done = bf16[1,32,32,128]{3,2,1,0:T(8,128)(2,1)S(1)} collective-permute-done((bf16[1,32,32,128]{3,2,1,0:T(8,128)(2,1)S(1)}, bf16[1,32,32,128]{3,2,1,0:T(8,128)(2,1)S(1)}, u32[]{:S(2)}, u32[]{:S(2)}) %collective-permute-start) | collective-permute-done | bytes 262176 | tf_op jit(solution)/shard_map/ppermute | solution.py:52
  177.7 3.5 %collective-permute-start.4 = (bf16[1,32,32,128]{3,2,1,0:T(8,128)(2,1)S(1)}, bf16[1,32,32,128]{3,2,1,0:T(8,128)(2,1)S(1)}, u32[]{:S(2)}, u32[]{:S(2)}) collective-permute-start(bf16[1,32,32,128]{3,2,1,0:T(8,128)(2,1)S(1)} %multiply_convert_fusion.1), channel_id=1, source_target_pairs={{0,7},{1,0},{2,1},{3,2},{4,3},{5,4},{6,5},{7,6},{8,15},{9,8},{10,9... | collective-permute-start | bytes 786440 | tf_op jit(solution)/shard_map/ppermute | solution.py:54
  181.2 4.2 %collective-permute-done.1 = bf16[1,32,32,128]{3,2,1,0:T(8,128)(2,1)S(1)} collective-permute-done((bf16[1,32,32,128]{3,2,1,0:T(8,128)(2,1)S(1)}, bf16[1,32,32,128]{3,2,1,0:T(8,128)(2,1)S(1)}, u32[]{:S(2)}, u32[]{:S(2)}) %collective-permute-start.1) | collective-permute-done | bytes 262176 | tf_op jit(solution)/shard_map/ppermute | solution.py:52
  185.5 3.7 %collective-permute-start.5 = (bf16[1,32,32,128]{3,2,1,0:T(8,128)(2,1)S(1)}, bf16[1,32,32,128]{3,2,1,0:T(8,128)(2,1)S(1)}, u32[]{:S(2)}, u32[]{:S(2)}) collective-permute-start(bf16[1,32,32,128]{3,2,1,0:T(8,128)(2,1)S(1)} %collective-permute-done.4), channel_id=1, source_target_pairs={{0,7},{1,0},{2,1},{3,2},{4,3},{5,4},{6,5},{7,6},{8,15},{9,8},{10,9... | collective-permute-start | bytes 786440 | tf_op jit(solution)/shard_map/ppermute | solution.py:54
  189.2 4.0 %collective-permute-done.2 = bf16[1,32,32,128]{3,2,1,0:T(8,128)(2,1)S(1)} collective-permute-done((bf16[1,32,32,128]{3,2,1,0:T(8,128)(2,1)S(1)}, bf16[1,32,32,128]{3,2,1,0:T(8,128)(2,1)S(1)}, u32[]{:S(2)}, u32[]{:S(2)}) %collective-permute-start.2) | collective-permute-done | bytes 262176 | tf_op jit(solution)/shard_map/ppermute | solution.py:52
  193.2 3.5 %collective-permute-start.6 = (bf16[1,32,32,128]{3,2,1,0:T(8,128)(2,1)S(1)}, bf16[1,32,32,128]{3,2,1,0:T(8,128)(2,1)S(1)}, u32[]{:S(2)}, u32[]{:S(2)}) collective-permute-start(bf16[1,32,32,128]{3,2,1,0:T(8,128)(2,1)S(1)} %collective-permute-done.5), channel_id=1, source_target_pairs={{0,7},{1,0},{2,1},{3,2},{4,3},{5,4},{6,5},{7,6},{8,15},{9,8},{10,9... | collective-permute-start | bytes 786440 | tf_op jit(solution)/shard_map/ppermute | solution.py:54
  196.8 4.0 %collective-permute-done.3 = bf16[1,32,32,128]{3,2,1,0:T(8,128)(2,1)S(1)} collective-permute-done((bf16[1,32,32,128]{3,2,1,0:T(8,128)(2,1)S(1)}, bf16[1,32,32,128]{3,2,1,0:T(8,128)(2,1)S(1)}, u32[]{:S(2)}, u32[]{:S(2)}) %collective-permute-start.3) | collective-permute-done | bytes 262176 | tf_op jit(solution)/shard_map/ppermute | solution.py:52
  203.3 2.9 %fusion.4 = bf16[3,3,128,1024,1]{3,2,0,1,4:T(8,128)(2,1)S(1)} fusion(bf16[32,32,3,3,128]{4,1,0,3,2:T(8,128)(2,1)S(1)} %bitcast.224, bf16[1,32,32,2048]{3,2,1,0:T(8,128)(2,1)S(1)} %constant_dynamic-update-slice_fusion, s32[]{:T(128)S(6)} %select_n.14), kind=kOutput, calls=%fused_computation.7 | convolution fusion | flops 2415919104 | bytes 6815748 | tf_op jit(solution)/shard_map/bhwc,bhwpqd->pqcd/dot_general | solution.py:39
  209.7 4.5 %fusion.13 = f32[1,32,32,3,3,128]{5,2,4,3,1,0:T(8,128)S(1)} fusion(bf16[3,3,1024,128]{3,2,1,0:T(8,128)(2,1)S(1)} %copy-done.5, bf16[1,32,32,2048]{3,2,1,0:T(8,128)(2,1)} %copy-done.4, s32[]{:T(128)S(6)} %select_n.14), kind=kOutput, calls=%fused_computation.14 | convolution fusion | flops 2415919104 | bytes 9175044 | tf_op jit(solution)/shard_map/bhwc,pqcd->bhwpqd/dot_general | solution.py:14
  216.2 2.3 copy.45
  218.5 27.8 %reduce-scatter.8.cloned.1.call-done = bf16[3,3,256,128]{2,3,1,0:T(8,128)(2,1)} async-done(((bf16[3,3,1024,128]{2,3,1,0:T(8,128)(2,1)}), bf16[3,3,256,128]{2,3,1,0:T(8,128)(2,1)}) %reduce-scatter.8.cloned.1.call-update) | async-done | bytes 589840 | tf_op jit(solution)/shard_map/reduce_scatter | solution.py:59
  246.2 2.3 copy.46
  (73 shorter events, 17.6 us)
Async XLA Ops:
  7.2 4.3 %copy-start = (bf16[1,32,32,128]{3,2,1,0:T(8,128)(2,1)S(1)}, bf16[1,32,32,128]{3,2,1,0:T(8,128)(2,1)}, u32[]{:S(2)}) copy-start(bf16[1,32,32,128]{3,2,1,0:T(8,128)(2,1)} %param.7) | copy-start | bytes 786436
  7.2 42.9 %all-gather.8.cloned.1.call-start = ((), (), s32[]{:S(2)}) async-start(), calls=%async_computation.5 | async-start | bytes 2949120 | tf_op jit(solution)/shard_map/all_gather | solution.py:57
  7.9 81.5 %all-gather.6.cloned.1.call-start = ((), (), s32[]{:S(2)}) async-start(), calls=%async_computation.4 | async-start | bytes 2949120 | tf_op jit(solution)/shard_map/all_gather | solution.py:43
  8.7 113.2 %all-gather.4.cloned.1.call-start = ((), (), s32[]{:S(2)}) async-start(), calls=%async_computation.3 | async-start | bytes 2359296 | tf_op jit(solution)/shard_map/all_gather | solution.py:44
  9.4 149.5 %reduce-scatter.10.cloned.1.call-start = ((), (), s32[]{:S(2)}) async-start(), calls=%async_computation.8 | async-start | bytes 2359296
  12.1 38.0 %copy-start.2 = (bf16[1,32,32,9,128]{4,2,1,3,0:T(8,128)(2,1)}, bf16[1,32,32,9,128]{4,2,1,3,0:T(8,128)(2,1)S(1)}, u32[]{:S(2)}) copy-start(bf16[1,32,32,9,128]{4,2,1,3,0:T(8,128)(2,1)S(1)} %fusion.57) | copy-start | bytes 7077892
  80.0 136.2 %reduce-scatter.6.cloned.1.call-start = ((), (), s32[]{:S(2)}) async-start(), calls=%async_computation.6 | async-start | bytes 2949120 | tf_op jit(solution)/shard_map/reduce_scatter | solution.py:71
  127.1 2.1 copy-start.1
  164.0 1.6 copy-start.6
  169.7 76.6 %reduce-scatter.8.cloned.1.call-start = ((), (), s32[]{:S(2)}) async-start(), calls=%async_computation.7 | async-start | bytes 2949120 | tf_op jit(solution)/shard_map/reduce_scatter | solution.py:59
  169.9 7.8 %collective-permute-start = (bf16[1,32,32,128]{3,2,1,0:T(8,128)(2,1)S(1)}, bf16[1,32,32,128]{3,2,1,0:T(8,128)(2,1)S(1)}, u32[]{:S(2)}, u32[]{:S(2)}) collective-permute-start(bf16[1,32,32,128]{3,2,1,0:T(8,128)(2,1)S(1)} %multiply_convert_fusion.1), channel_id=1, source_target_pairs={{0,1},{1,2},{2,3},{3,4},{4,5},{5,6},{6,7},{7,0},{8,9},{9,10},{10,1... | collective-permute-start | bytes 786440 | tf_op jit(solution)/shard_map/ppermute | solution.py:52
  177.7 7.8 %collective-permute-start.1 = (bf16[1,32,32,128]{3,2,1,0:T(8,128)(2,1)S(1)}, bf16[1,32,32,128]{3,2,1,0:T(8,128)(2,1)S(1)}, u32[]{:S(2)}, u32[]{:S(2)}) collective-permute-start(bf16[1,32,32,128]{3,2,1,0:T(8,128)(2,1)S(1)} %collective-permute-done), channel_id=1, source_target_pairs={{0,1},{1,2},{2,3},{3,4},{4,5},{5,6},{6,7},{7,0},{8,9},{9,10},{10,1... | collective-permute-start | bytes 786440 | tf_op jit(solution)/shard_map/ppermute | solution.py:52
  177.7 7.8 %collective-permute-start.4 = (bf16[1,32,32,128]{3,2,1,0:T(8,128)(2,1)S(1)}, bf16[1,32,32,128]{3,2,1,0:T(8,128)(2,1)S(1)}, u32[]{:S(2)}, u32[]{:S(2)}) collective-permute-start(bf16[1,32,32,128]{3,2,1,0:T(8,128)(2,1)S(1)} %multiply_convert_fusion.1), channel_id=1, source_target_pairs={{0,7},{1,0},{2,1},{3,2},{4,3},{5,4},{6,5},{7,6},{8,15},{9,8},{10,9... | collective-permute-start | bytes 786440 | tf_op jit(solution)/shard_map/ppermute | solution.py:54
  185.5 7.8 %collective-permute-start.2 = (bf16[1,32,32,128]{3,2,1,0:T(8,128)(2,1)S(1)}, bf16[1,32,32,128]{3,2,1,0:T(8,128)(2,1)S(1)}, u32[]{:S(2)}, u32[]{:S(2)}) collective-permute-start(bf16[1,32,32,128]{3,2,1,0:T(8,128)(2,1)S(1)} %collective-permute-done.1), channel_id=1, source_target_pairs={{0,1},{1,2},{2,3},{3,4},{4,5},{5,6},{6,7},{7,0},{8,9},{9,10},{10,1... | collective-permute-start | bytes 786440 | tf_op jit(solution)/shard_map/ppermute | solution.py:52
  185.5 7.8 %collective-permute-start.5 = (bf16[1,32,32,128]{3,2,1,0:T(8,128)(2,1)S(1)}, bf16[1,32,32,128]{3,2,1,0:T(8,128)(2,1)S(1)}, u32[]{:S(2)}, u32[]{:S(2)}) collective-permute-start(bf16[1,32,32,128]{3,2,1,0:T(8,128)(2,1)S(1)} %collective-permute-done.4), channel_id=1, source_target_pairs={{0,7},{1,0},{2,1},{3,2},{4,3},{5,4},{6,5},{7,6},{8,15},{9,8},{10,9... | collective-permute-start | bytes 786440 | tf_op jit(solution)/shard_map/ppermute | solution.py:54
  193.2 7.6 %collective-permute-start.3 = (bf16[1,32,32,128]{3,2,1,0:T(8,128)(2,1)S(1)}, bf16[1,32,32,128]{3,2,1,0:T(8,128)(2,1)S(1)}, u32[]{:S(2)}, u32[]{:S(2)}) collective-permute-start(bf16[1,32,32,128]{3,2,1,0:T(8,128)(2,1)S(1)} %collective-permute-done.2), channel_id=1, source_target_pairs={{0,1},{1,2},{2,3},{3,4},{4,5},{5,6},{6,7},{7,0},{8,9},{9,10},{10,1... | collective-permute-start | bytes 786440 | tf_op jit(solution)/shard_map/ppermute | solution.py:52
  193.2 8.3 %collective-permute-start.6 = (bf16[1,32,32,128]{3,2,1,0:T(8,128)(2,1)S(1)}, bf16[1,32,32,128]{3,2,1,0:T(8,128)(2,1)S(1)}, u32[]{:S(2)}, u32[]{:S(2)}) collective-permute-start(bf16[1,32,32,128]{3,2,1,0:T(8,128)(2,1)S(1)} %collective-permute-done.5), channel_id=1, source_target_pairs={{0,7},{1,0},{2,1},{3,2},{4,3},{5,4},{6,5},{7,6},{8,15},{9,8},{10,9... | collective-permute-start | bytes 786440 | tf_op jit(solution)/shard_map/ppermute | solution.py:54
  201.6 1.7 copy-start.3
  203.3 2.9 %copy-start.4 = (bf16[1,32,32,2048]{3,2,1,0:T(8,128)(2,1)}, bf16[1,32,32,2048]{3,2,1,0:T(8,128)(2,1)S(1)}, u32[]{:S(2)}) copy-start(bf16[1,32,32,2048]{3,2,1,0:T(8,128)(2,1)S(1)} %constant_dynamic-update-slice_fusion) | copy-start | bytes 12582916
  208.0 1.7 copy-start.5
Sparse Core Ops, SparseCore 0:
  9.9 40.1 all-gather.7
  51.9 37.4 all-gather.5
  91.0 30.8 all-gather.3
  124.0 34.8 reduce-scatter.9
  169.8 36.0 reduce-scatter.5
  208.8 37.3 reduce-scatter.7
